TPU v7x, 128 devices: a whole 4x4x4 slice. The times are simulated.
128 devices in a mesh: row: 8 (over y, core), col: 16 (over z, x).
Axes of the slice: x: 4, y: 4, z: 4, core: 2. Of those that a mesh axis runs over, the one named last changes fastest.
Arguments:
- wavefunction: bfloat16 [32, 16, 256, 256], P('row', 'col'), may hold values from -6 to 6
- env_left: bfloat16 [16, 32, 2, 256, 256], P('col', 'row'), may hold values from -0.25 to 0.25
- left_src: int32 [16, 32, 2], P('col', 'row'), may hold values from 0 to 3
- two_site: bfloat16 [16, 16, 16], P('col'), may hold values from -1.5 to 1.5
- env_right: bfloat16 [16, 32, 256, 256], P('col', 'row'), may hold values from -0.09375 to 0.09375
- right_loc: int32 [32, 16], P('row', 'col'), may hold values from 0 to 3
- left_size: int32 [32], P('row'), may hold values from 128 to 256
- right_size: int32 [32], P('row'), may hold values from 128 to 256
Outputs:
- applied: bfloat16 [32, 16, 256, 256], P('row', 'col')
All inputs are finite; a program needn't handle non-finite values.
Results may differ from a plain program's by a relative error of at most 0.018.
Values may be sent and summed in bfloat16 or wider, within the bound.
No kernel may reach another device: no remote copies, remote signals or barrier semaphores. Data moves between devices by JAX's collectives and lax.ppermute only.
A program may use at most 128 MiB of HBM per device.

v0:
```python
import jax
import jax.numpy as jnp
from jax import lax
from jax.sharding import PartitionSpec as P


def per_device(
    wavefunction, env_left, left_src, two_site, env_right, right_loc, left_size, right_size
):
    whole, whole_loc = (
        lax.all_gather(wavefunction, "col", axis=1, tiled=True),
        lax.all_gather(right_loc, "col", axis=1, tiled=True),
    )
    local_tiles = wavefunction.shape[0]
    tile_width = wavefunction.shape[3]
    mixed_rows = []
    for position in range(local_tiles):
        blocks = whole[left_src[0, position]]
        left_part = jnp.einsum(
            "kxy,ksyz->sxz", env_left[0, position], blocks, preferred_element_type=jnp.float32
        ).astype(jnp.bfloat16)
        mixed_rows.append(
            jnp.einsum(
                "ts,sxz->txz", two_site[0], left_part, preferred_element_type=jnp.float32
            ).astype(jnp.bfloat16)
        )
    mixed = jnp.stack(mixed_rows)
    col_iota = lax.broadcasted_iota(jnp.int32, (1, 1, tile_width), 2)
    received, recv_loc = (
        lax.all_to_all(mixed, "row", split_axis=1, concat_axis=0, tiled=True),
        lax.all_to_all(whole_loc, "row", split_axis=1, concat_axis=0, tiled=True),
    )
    pieces = []
    for column in range(received.shape[1]):
        chosen = env_right[0][recv_loc[:, column]]
        product = jnp.einsum(
            "axy,azy->axz", received[:, column], chosen, preferred_element_type=jnp.float32
        )
        col_limit = right_size[recv_loc[:, column]]
        inside = col_iota < col_limit[:, None, None]
        pieces.append(jnp.where(inside, product, 0.0).astype(jnp.bfloat16))
    term = lax.all_to_all(jnp.stack(pieces, axis=1), "row", split_axis=0, concat_axis=1, tiled=True)
    summed = lax.psum_scatter(
        term.astype(jnp.float32).astype(jnp.bfloat16), "col", scatter_dimension=1, tiled=True
    ).astype(jnp.float32)
    row_iota = lax.broadcasted_iota(jnp.int32, summed.shape, 2)
    inside_rows = row_iota < left_size[:, None, None, None]
    return jnp.where(inside_rows, summed, 0.0).astype(jnp.bfloat16)


def solution(mesh):
    placed = (
        P("row", "col", None, None),
        P("col", "row", None, None, None),
        P("col", "row", None),
        P("col", None, None),
        P("col", "row", None, None),
        P("row", "col"),
        P("row"),
        P("row"),
    )
    return jax.shard_map(
        per_device,
        mesh=mesh,
        in_specs=placed,
        out_specs=P("row", "col", None, None),
        check_vma=False,
    )
```

profile of v0, /device:TPU:1, one launch (start us, length us, event | category | flops | bytes accessed | tf_op | source)
XLA Modules:
  0.0 596.2 jit_solution(1501007717909477833)
XLA Ops:
  6.5 0.0 copy-start
  6.5 0.7 all-gather.3.cloned.1.call-update
  7.3 18.3 %all-gather = s32[16,1,4]{2,1,0:T(1,128)S(1)} all-gather(s32[1,1,4]{2,1,0:T(1,128)} %bitcast.158), channel_id=1, replica_groups=mesh['row'=8,'col'=16] {'col'}, dimensions={0}, use_global_device_ids=true | all-gather | bytes 272 | tf_op jit(solution)/shard_map/all_gather | solution.py:12
  25.5 0.1 copy.30
  25.6 0.7 copy.31
  26.3 9.6 %all-to-all-start = ((s32[4,8,2]{0,2,1:T(2,128)}), s32[4,8,2]{0,2,1:T(2,128)S(1)}, u32[]{:S(2)}, u32[]{:S(2)}) async-start(s32[4,8,2]{0,2,1:T(2,128)} %bitcast.3), calls=%async_computation | async-start | bytes 16384 | tf_op jit(solution)/shard_map/all_to_all | solution.py:31
  35.9 1.0 slice_reduce_fusion.3
  37.0 46.7 %all-gather.3.cloned.1.call-done = bf16[4,16,256,256]{3,2,1,0:T(8,128)(2,1)} async-done(((bf16[4,1,256,256]{3,2,1,0:T(8,128)(2,1)}), bf16[4,16,256,256]{3,2,1,0:T(8,128)(2,1)}) %all-gather.3.cloned.1.call-update) | async-done | bytes 8388624 | tf_op jit(solution)/shard_map/all_gather | solution.py:11
  83.7 6.0 fusion.62
  89.6 2.9 gather_fusion.6
  92.5 4.2 gather_fusion.7
  96.7 4.2 gather_fusion.4
  100.9 4.2 gather_fusion.5
  105.1 4.2 gather_fusion.2
  109.3 4.2 gather_fusion.3
  113.6 4.2 gather_fusion.8
  117.8 4.2 gather_fusion.9
  122.0 2.4 copy.39
  124.4 4.1 copy.40
  128.5 4.2 fusion.34
  132.7 3.3 copy.41
  136.0 4.0 copy.36
  140.0 4.0 copy.37
  144.0 4.9 fusion.31
  148.8 4.6 copy.38
  153.4 2.1 convert_bitcast_fusion.1
  155.5 2.0 convert_bitcast_fusion.2
  157.5 3.9 copy.33
  161.5 2.4 copy.34
  163.8 4.9 fusion.28
  168.7 3.3 copy.35
  172.1 2.0 convert_bitcast_fusion.3
  174.1 4.1 copy.42
  178.2 0.0 copy-done.3
  178.2 2.4 copy.43
  180.6 4.9 fusion.37
  185.4 3.3 copy.44
  188.8 0.7 convert_bitcast_fusion
  189.5 0.9 copy-done.5
  190.4 0.6 copy-done.6
  191.0 5.7 pad_maximum_fusion
  196.7 9.6 %copy.45 = bf16[4,16,256,256]{3,2,0,1:T(8,128)(2,1)} copy(bf16[4,16,256,256]{3,1,2,0:T(8,128)(2,1)} %pad_maximum_fusion) | data formatting | bytes 16777216 | tf_op jit(solution)/shard_map/stack | solution.py:27
  206.3 0.0 all-to-all-done
  206.3 5.6 all-to-all-start.1
  212.0 0.6 fusion.63
  212.6 0.1 all_to_all.43
  212.7 2.8 gather_fusion
  215.5 2.8 gather_fusion.1
  218.3 2.5 compare_select_fusion.9
  220.8 0.1 iota_compare_fusion.1
  220.9 85.0 %all-to-all-done.1 = bf16[4,16,256,256]{3,2,0,1:T(8,128)(2,1)} async-done(((bf16[4,16,256,256]{3,2,0,1:T(8,128)(2,1)}), bf16[4,16,256,256]{3,2,0,1:T(8,128)(2,1)}, u32[]{:S(2)}, u32[]{:S(2)}) %all-to-all-start.1) | async-done | bytes 8388640 | tf_op jit(solution)/shard_map/all_to_all | solution.py:30
  305.9 7.8 %copy.46 = bf16[4,8,2,256,256]{4,3,0,1,2:T(8,128)(2,1)} copy(bf16[4,8,2,256,256]{4,3,0,2,1:T(8,128)(2,1)} %bitcast.44) | data formatting | bytes 16777216 | tf_op jit(solution)/shard_map/all_to_all | solution.py:30
  313.6 5.8 fusion
  319.4 1.5 copy-done.7
  321.0 3.3 fusion.1
  324.2 6.2 %pad_maximum_fusion.1 = bf16[32,2,256,256]{3,2,0,1:T(8,128)(2,1)} fusion(bf16[32,1,256,256]{3,2,0,1:T(8,128)(2,1)} %fusion.1, bf16[32,1,256,256]{3,2,0,1:T(8,128)(2,1)S(1)} %copy-done.9), kind=kLoop, calls=%fused_computation.11 | loop fusion | flops 4194304 | bytes 16777216 | tf_op jit(solution)/shard_map/stack | solution.py:42
  330.4 7.6 %copy.47 = bf16[32,2,256,256]{3,2,1,0:T(8,128)(2,1)} copy(bf16[32,2,256,256]{3,2,0,1:T(8,128)(2,1)} %pad_maximum_fusion.1) | data formatting | bytes 16777216 | tf_op jit(solution)/shard_map/stack | solution.py:42
  338.0 101.5 %all_to_all.55 = bf16[32,2,256,256]{3,2,1,0:T(8,128)(2,1)} all-to-all(bf16[32,2,256,256]{3,2,1,0:T(8,128)(2,1)} %copy.47), channel_id=1, replica_groups=mesh['row'=8,'col'=16] {'row'}, dimensions={0} | all-to-all | bytes 16777216 | tf_op jit(solution)/shard_map/all_to_all | solution.py:42
  439.5 7.6 %copy.48 = bf16[4,8,2,256,256]{4,3,2,1,0:T(8,128)(2,1)} copy(bf16[4,8,2,256,256]{4,3,2,0,1:T(8,128)(2,1)} %bitcast.153) | data formatting | bytes 16777216 | tf_op jit(solution)/shard_map/all_to_all | solution.py:42
  447.1 0.0 all-reduce.3.cloned.1.call-update
  447.2 0.6 copy-done.14
  447.8 0.6 dynamic-slice
  448.4 138.3 %all-reduce.3.cloned.1.call-done = bf16[4,16,256,256]{3,2,1,0:T(8,128)(2,1)} async-done(((bf16[4,16,256,256]{3,2,1,0:T(8,128)(2,1)}), bf16[4,16,256,256]{3,2,1,0:T(8,128)(2,1)}) %all-reduce.3.cloned.1.call-update) | async-done | bytes 8388624
  586.7 2.7 select_convert_fusion.2
  (35 shorter events, 0.1 us)
Async XLA Ops:
  6.5 206.2 %copy-start = (bf16[1,4,256,256]{3,2,1,0:T(8,128)(2,1)S(1)}, bf16[1,4,256,256]{3,2,1,0:T(8,128)(2,1)}, u32[]{:S(2)}) copy-start(bf16[1,4,256,256]{3,2,1,0:T(8,128)(2,1)} %param.12) | copy-start | bytes 1572868
  6.5 77.1 %all-gather.3.cloned.1.call-start = ((), (), s32[]{:S(2)}) async-start(), calls=%async_computation.3 | async-start | bytes 8912896 | tf_op jit(solution)/shard_map/all_gather | solution.py:11
  26.3 180.1 %all-to-all-start = ((s32[4,8,2]{0,2,1:T(2,128)}), s32[4,8,2]{0,2,1:T(2,128)S(1)}, u32[]{:S(2)}, u32[]{:S(2)}) async-start(s32[4,8,2]{0,2,1:T(2,128)} %bitcast.3), calls=%async_computation | async-start | bytes 16384 | tf_op jit(solution)/shard_map/all_to_all | solution.py:31
  124.4 4.1 copy-start.10
  148.8 4.6 copy-start.11
  153.4 2.1 copy-start.1
  155.5 6.0 copy-start.4
  174.1 4.1 copy-start.3
  188.8 1.6 copy-start.5
  188.8 2.2 copy-start.6
  206.3 5.6 copy-start.12
  206.3 99.5 %all-to-all-start.1 = ((bf16[4,16,256,256]{3,2,0,1:T(8,128)(2,1)}), bf16[4,16,256,256]{3,2,0,1:T(8,128)(2,1)}, u32[]{:S(2)}, u32[]{:S(2)}) async-start(bf16[4,16,256,256]{3,2,0,1:T(8,128)(2,1)} %copy.45), calls=%async_computation.1 | async-start | bytes 16777216 | tf_op jit(solution)/shard_map/all_to_all | solution.py:30
  212.0 374.7 %all-reduce.3.cloned.1.call-start = ((), (), s32[]{:S(2)}) async-start(), calls=%async_computation.4 | async-start | bytes 16777216
  305.8 7.8 %copy-start.8 = (bf16[32,256,256]{2,1,0:T(8,128)(2,1)S(1)}, bf16[32,256,256]{2,1,0:T(8,128)(2,1)}, u32[]{:S(2)}) copy-start(bf16[32,256,256]{2,1,0:T(8,128)(2,1)} %gather_fusion) | copy-start | bytes 12582916
  313.6 5.8 copy-start.2
  313.6 7.3 %copy-start.7 = (bf16[32,256,256]{2,1,0:T(8,128)(2,1)S(1)}, bf16[32,256,256]{2,1,0:T(8,128)(2,1)}, u32[]{:S(2)}) copy-start(bf16[32,256,256]{2,1,0:T(8,128)(2,1)} %gather_fusion.1) | copy-start | bytes 12582916
  321.0 3.3 copy-start.9
  447.1 0.7 copy-start.14
  447.1 139.6 %copy-start.13 = (s32[4]{0:T(128)S(1)}, s32[4]{0:T(128)}, u32[]{:S(2)}) copy-start(s32[4]{0:T(128)} %param.14) | copy-start | bytes 52
Sparse Core Ops, SparseCore 0:
  9.5 74.1 all-gather.2
  447.3 139.3 all-reduce.2
where the time goes:
time: 598 us; the launch traced here: 596 us
  waiting for transfers between devices  271 us (45%)
  local copies, waits for them, and re-layouts  125 us (21%)
  blocking collectives  120 us (20%)
  matrix products  34.7 us (6%)
  other arithmetic  17.2 us (3%)
  starting transfers between devices  15.2 us (3%)
  between operations  13.6 us (2%)
    unnamed x3, waiting for transfers between devices  139 us
    all_to_all x1, blocking collectives, per_device(): lax.all_to_all(jnp.stack(pieces, axis=1), 'row', split_axis=0, concat_axi...  101 us
    all_to_all x1, waiting for transfers between devices, per_device(): lax.all_to_all(mixed, 'row', split_axis=1, concat_axis=0, tiled=True)  85 us
    gather x17, local copies, waits for them, and re-layouts, per_device(): blocks = whole[left_src[0, position]]  65.5 us
    all_gather x1, waiting for transfers between devices, per_device(): lax.all_gather(wavefunction, 'col', axis=1, tiled=True)  46.7 us
    dot_general x4, matrix products, per_device(): jnp.einsum('kxy,ksyz->sxz', env_left[0, position], blocks, preferred_elem...  18.8 us
    all_gather x1, blocking collectives, per_device(): lax.all_gather(right_loc, 'col', axis=1, tiled=True)  18.3 us
    convert_element_type x4, local copies, waits for them, and re-layouts, per_device(): left_part = jnp.einsum('kxy,ksyz->sxz', env_left[0, position], blocks, pr...  14.6 us
  transfers between devices with their start and end apart: 4, of which 3 were waited for; matrix products, arithmetic and copies ran while one was open for 22% of the time, Pallas kernels for 0%

commit v1 on v0

--- a/solution.py
+++ b/solution.py
@@ -1,14 +1,41 @@
+import functools
 import jax
 import jax.numpy as jnp
 from jax import lax
 from jax.sharding import PartitionSpec as P
+from jax.lax import axis_index, axis_size, ppermute
+
+
+def arrange_copies(body, row_axis):
+    current_value = axis_size(row_axis)
+    step_out, current_arr, new = (current_value, axis_index(row_axis), body.shape[1])
+    all_rows = [(rr, (rr + 1) % step_out) for rr in range(step_out)]
+    by_rank = [(rr, (rr - 1) % step_out) for rr in range(step_out)]
+    current_block = jnp.zeros((*body.shape[:1], step_out * new, *body.shape[2:]), body.dtype)
+    current_block = lax.dynamic_update_slice_in_dim(current_block, body, current_arr * new, axis=1)
+    raw_out = tile_out = body
+    frame_out = step_out // 2
+    for i in [*range(1, frame_out + 1)]:
+        raw_out = ppermute(raw_out, row_axis, all_rows)
+        current_block = lax.dynamic_update_slice_in_dim(
+            current_block, raw_out, (current_arr - i) % step_out * new, axis=1
+        )
+        if i < step_out - frame_out:
+            tile_out = ppermute(tile_out, row_axis, by_rank)
+            current_block = lax.dynamic_update_slice_in_dim(
+                current_block, tile_out, (current_arr + i) % step_out * new, axis=1
+            )
+    return current_block
+
+
+screen_press = functools.partial(arrange_copies, row_axis="col")
 
 
 def per_device(
     wavefunction, env_left, left_src, two_site, env_right, right_loc, left_size, right_size
 ):
     whole, whole_loc = (
-        lax.all_gather(wavefunction, "col", axis=1, tiled=True),
+        screen_press(wavefunction),
         lax.all_gather(right_loc, "col", axis=1, tiled=True),
     )
     local_tiles = wavefunction.shape[0]

time: 598 us -> 672 us (1.12)
  starting transfers between devices: 15.2 us -> 53.5 us
  local copies, waits for them, and re-layouts: 125 us -> 149 us
  waiting for transfers between devices: 271 us -> 278 us
    ppermute x0 -> x15, waiting for transfers between devices: none -> 57.6 us  [the longest x8 38.7 us: arrange_copies(): raw_out = ppermute(raw_out, row_axis, all_rows)]
    all_gather x1 -> x0, waiting for transfers between devices: 46.7 us -> none  [per_device(): lax.all_gather(wavefunction, 'col', axis=1, tiled=True)]
    ppermute x0 -> x15, starting transfers between devices: none -> 33.2 us  [the longest x7 30.4 us: arrange_copies(): tile_out = ppermute(tile_out, row_axis, by_rank)]
    dynamic_update_slice x0 -> x16, local copies, waits for them, and re-layouts: none -> 19.4 us  [the longest x8 10.8 us: arrange_copies(): lax.dynamic_update_slice_in_dim(current_block, raw_out, (current_arr - i)...]
    unnamed x3 -> x2, waiting for transfers between devices: 139 us -> 135 us
  transfers between devices with their start and end apart: 4 -> 18, of which waited for: 3 -> 10; matrix products, arithmetic and copies ran while one was open for 22% -> 23% of each run, Pallas kernels for 0% -> 0%
where the time goes in v1:
time: 672 us; the launch traced here: 670 us
  waiting for transfers between devices  278 us (41%)
  local copies, waits for them, and re-layouts  149 us (22%)
  blocking collectives  124 us (18%)
  starting transfers between devices  53.5 us (8%)
  matrix products  34.6 us (5%)
  other arithmetic  17.2 us (3%)
  between operations  13.8 us (2%)
    unnamed x2, waiting for transfers between devices  135 us
    all_to_all x1, blocking collectives, per_device(): lax.all_to_all(jnp.stack(pieces, axis=1), 'row', split_axis=0, concat_axi...  101 us
    all_to_all x1, waiting for transfers between devices, per_device(): lax.all_to_all(mixed, 'row', split_axis=1, concat_axis=0, tiled=True)  85.1 us
    gather x17, local copies, waits for them, and re-layouts, per_device(): blocks = whole[left_src[0, position]]  65.7 us
    ppermute x8, waiting for transfers between devices, arrange_copies(): raw_out = ppermute(raw_out, row_axis, all_rows)  38.7 us
    ppermute x7, starting transfers between devices, arrange_copies(): tile_out = ppermute(tile_out, row_axis, by_rank)  30.4 us
    all_gather x1, blocking collectives, per_device(): lax.all_gather(right_loc, 'col', axis=1, tiled=True)  22.4 us
    ppermute x7, waiting for transfers between devices, arrange_copies(): tile_out = ppermute(tile_out, row_axis, by_rank)  18.9 us
  transfers between devices with their start and end apart: 18, of which 10 were waited for; matrix products, arithmetic and copies ran while one was open for 23% of the time, Pallas kernels for 0%

profile of v1, /device:TPU:1, one launch (start us, length us, event | category | flops | bytes accessed | tf_op | source)
XLA Modules:
  0.0 669.9 jit_solution(13849782225983410280)
XLA Ops:
  6.5 2.0 collective-permute-start
  8.6 4.7 collective-permute-start.1
  13.3 11.9 %collective-permute-done = bf16[4,1,256,256]{3,2,1,0:T(8,128)(2,1)S(1)} collective-permute-done((bf16[4,1,256,256]{3,2,1,0:T(8,128)(2,1)}, bf16[4,1,256,256]{3,2,1,0:T(8,128)(2,1)S(1)}, u32[]{:S(2)}, u32[]{:S(2)}) %collective-permute-start) | collective-permute-done | bytes 524320 | tf_op jit(solution)/shard_map/ppermute | solution.py:19
  25.2 4.8 collective-permute-start.3
  30.0 10.7 %collective-permute-done.2 = bf16[4,1,256,256]{3,2,1,0:T(8,128)(2,1)S(1)} collective-permute-done((bf16[4,1,256,256]{3,2,1,0:T(8,128)(2,1)S(1)}, bf16[4,1,256,256]{3,2,1,0:T(8,128)(2,1)S(1)}, u32[]{:S(2)}, u32[]{:S(2)}) %collective-permute-start.2) | collective-permute-done | bytes 524320 | tf_op jit(solution)/shard_map/ppermute | solution.py:19
  40.7 4.8 collective-permute-start.5
  45.5 9.8 %collective-permute-done.4 = bf16[4,1,256,256]{3,2,1,0:T(8,128)(2,1)S(1)} collective-permute-done((bf16[4,1,256,256]{3,2,1,0:T(8,128)(2,1)S(1)}, bf16[4,1,256,256]{3,2,1,0:T(8,128)(2,1)S(1)}, u32[]{:S(2)}, u32[]{:S(2)}) %collective-permute-start.4) | collective-permute-done | bytes 524320 | tf_op jit(solution)/shard_map/ppermute | solution.py:19
  55.3 22.4 %all-gather = s32[16,1,4]{2,1,0:T(1,128)S(1)} all-gather(s32[1,1,4]{2,1,0:T(1,128)} %bitcast.158), channel_id=1, replica_groups=mesh['row'=8,'col'=16] {'col'}, dimensions={0}, use_global_device_ids=true | all-gather | bytes 272 | tf_op jit(solution)/shard_map/all_gather | solution.py:39
  78.4 11.5 %all-to-all-start = ((s32[4,8,2]{0,2,1:T(2,128)}), s32[4,8,2]{0,2,1:T(2,128)S(1)}, u32[]{:S(2)}, u32[]{:S(2)}) async-start(s32[4,8,2]{0,2,1:T(2,128)} %bitcast.3), calls=%async_computation | async-start | bytes 16384 | tf_op jit(solution)/shard_map/all_to_all | solution.py:58
  92.6 4.3 broadcast_in_dim.37
  97.7 7.0 %collective-permute-done.7 = bf16[4,1,256,256]{3,2,1,0:T(8,128)(2,1)} collective-permute-done((bf16[4,1,256,256]{3,2,1,0:T(8,128)(2,1)S(1)}, bf16[4,1,256,256]{3,2,1,0:T(8,128)(2,1)}, u32[]{:S(2)}, u32[]{:S(2)}) %collective-permute-start.7) | collective-permute-done | bytes 524320 | tf_op jit(solution)/shard_map/ppermute | solution.py:24
  104.7 4.2 collective-permute-start.9
  111.0 1.9 constant_dynamic-update-slice_fusion.12
  112.8 6.9 %collective-permute-done.9 = bf16[4,1,256,256]{3,2,1,0:T(8,128)(2,1)} collective-permute-done((bf16[4,1,256,256]{3,2,1,0:T(8,128)(2,1)}, bf16[4,1,256,256]{3,2,1,0:T(8,128)(2,1)}, u32[]{:S(2)}, u32[]{:S(2)}) %collective-permute-start.9) | collective-permute-done | bytes 524320 | tf_op jit(solution)/shard_map/ppermute | solution.py:24
  119.7 5.5 collective-permute-start.11
  127.7 1.9 constant_dynamic-update-slice_fusion.8
  131.4 3.6 collective-permute-done.11
  135.1 5.4 collective-permute-start.13
  140.5 1.9 constant_dynamic-update-slice_fusion.6
  149.9 6.3 collective-permute-done.14
  157.0 6.0 fusion.62
  163.1 2.9 gather_fusion.2
  165.9 4.2 gather_fusion.3
  170.2 4.2 gather_fusion.4
  174.4 4.2 gather_fusion.5
  178.6 4.3 gather_fusion.6
  182.8 4.2 gather_fusion.7
  187.1 4.2 gather_fusion.8
  191.3 4.2 gather_fusion.9
  195.5 2.4 copy.33
  197.9 4.1 copy.34
  202.0 4.2 fusion.28
  206.2 3.3 copy.35
  209.6 4.0 copy.36
  213.6 4.0 copy.37
  217.5 4.8 fusion.31
  222.3 4.6 copy.38
  226.9 2.0 convert_bitcast_fusion.3
  229.0 2.0 convert_bitcast_fusion.2
  231.0 4.0 copy.39
  235.0 2.4 copy.40
  237.4 4.9 fusion.34
  242.3 3.3 copy.41
  245.6 2.1 convert_bitcast_fusion.1
  247.7 4.1 copy.42
  251.8 2.4 copy.43
  254.1 4.8 fusion.37
  259.0 3.3 copy.44
  264.5 5.7 pad_maximum_fusion
  270.3 9.7 %copy.45 = bf16[4,16,256,256]{3,2,0,1:T(8,128)(2,1)} copy(bf16[4,16,256,256]{3,1,2,0:T(8,128)(2,1)} %pad_maximum_fusion) | data formatting | bytes 16777216 | tf_op jit(solution)/shard_map/stack | solution.py:54
  280.0 8.8 %all-to-all-start.1 = ((bf16[4,16,256,256]{3,2,0,1:T(8,128)(2,1)}), bf16[4,16,256,256]{3,2,0,1:T(8,128)(2,1)}, u32[]{:S(2)}, u32[]{:S(2)}) async-start(bf16[4,16,256,256]{3,2,0,1:T(8,128)(2,1)} %copy.45), calls=%async_computation.1 | async-start | bytes 16777216 | tf_op jit(solution)/shard_map/all_to_all | solution.py:57
  289.5 2.8 gather_fusion
  292.3 2.8 gather_fusion.1
  295.1 2.3 compare_select_fusion.9
  297.5 85.1 %all-to-all-done.1 = bf16[4,16,256,256]{3,2,0,1:T(8,128)(2,1)} async-done(((bf16[4,16,256,256]{3,2,0,1:T(8,128)(2,1)}), bf16[4,16,256,256]{3,2,0,1:T(8,128)(2,1)}, u32[]{:S(2)}, u32[]{:S(2)}) %all-to-all-start.1) | async-done | bytes 8388640 | tf_op jit(solution)/shard_map/all_to_all | solution.py:57
  382.6 7.8 %copy.46 = bf16[4,8,2,256,256]{4,3,0,1,2:T(8,128)(2,1)} copy(bf16[4,8,2,256,256]{4,3,0,2,1:T(8,128)(2,1)} %bitcast.44) | data formatting | bytes 16777216 | tf_op jit(solution)/shard_map/all_to_all | solution.py:57
  390.4 5.8 fusion
  397.8 3.2 fusion.1
  401.0 6.2 pad_maximum_fusion.1
  407.3 7.6 %copy.47 = bf16[32,2,256,256]{3,2,1,0:T(8,128)(2,1)} copy(bf16[32,2,256,256]{3,2,0,1:T(8,128)(2,1)} %pad_maximum_fusion.1) | data formatting | bytes 16777216 | tf_op jit(solution)/shard_map/stack | solution.py:69
  414.9 101.5 %all_to_all.55 = bf16[32,2,256,256]{3,2,1,0:T(8,128)(2,1)} all-to-all(bf16[32,2,256,256]{3,2,1,0:T(8,128)(2,1)} %copy.47), channel_id=1, replica_groups=mesh['row'=8,'col'=16] {'row'}, dimensions={0} | all-to-all | bytes 16777216 | tf_op jit(solution)/shard_map/all_to_all | solution.py:69
  516.3 7.7 %copy.48 = bf16[4,8,2,256,256]{4,3,2,1,0:T(8,128)(2,1)} copy(bf16[4,8,2,256,256]{4,3,2,0,1:T(8,128)(2,1)} %bitcast.153) | data formatting | bytes 16777216 | tf_op jit(solution)/shard_map/all_to_all | solution.py:69
  525.3 135.0 %all-reduce.3.cloned.1.call-done = bf16[4,16,256,256]{3,2,1,0:T(8,128)(2,1)} async-done(((bf16[4,16,256,256]{3,2,1,0:T(8,128)(2,1)}), bf16[4,16,256,256]{3,2,1,0:T(8,128)(2,1)}) %all-reduce.3.cloned.1.call-update) | async-done | bytes 8388624
  660.3 2.8 select_convert_fusion.2
  (83 shorter events, 24.6 us)
Async XLA Ops:
  6.5 282.9 %copy-start = (bf16[1,4,256,256]{3,2,1,0:T(8,128)(2,1)S(1)}, bf16[1,4,256,256]{3,2,1,0:T(8,128)(2,1)}, u32[]{:S(2)}) copy-start(bf16[1,4,256,256]{3,2,1,0:T(8,128)(2,1)} %param.12) | copy-start | bytes 1572868
  6.5 18.6 %collective-permute-start = (bf16[4,1,256,256]{3,2,1,0:T(8,128)(2,1)}, bf16[4,1,256,256]{3,2,1,0:T(8,128)(2,1)S(1)}, u32[]{:S(2)}, u32[]{:S(2)}) collective-permute-start(bf16[4,1,256,256]{3,2,1,0:T(8,128)(2,1)} %param.8), channel_id=1, source_target_pairs={{0,1},{1,2},{2,3},{3,4},{4,5},{5,6},{6,7},{7,8},{8,9},{9,10},{10,1... | collective-permute-start | bytes 1572872 | tf_op jit(solution)/shard_map/ppermute | solution.py:19
  8.6 16.6 %collective-permute-start.1 = (bf16[4,1,256,256]{3,2,1,0:T(8,128)(2,1)}, bf16[4,1,256,256]{3,2,1,0:T(8,128)(2,1)S(1)}, u32[]{:S(2)}, u32[]{:S(2)}) collective-permute-start(bf16[4,1,256,256]{3,2,1,0:T(8,128)(2,1)} %param.8), channel_id=1, source_target_pairs={{0,15},{1,0},{2,1},{3,2},{4,3},{5,4},{6,5},{7,6},{8,7},{9,8},{10,9... | collective-permute-start | bytes 1572872 | tf_op jit(solution)/shard_map/ppermute | solution.py:24
  25.2 15.5 %collective-permute-start.2 = (bf16[4,1,256,256]{3,2,1,0:T(8,128)(2,1)S(1)}, bf16[4,1,256,256]{3,2,1,0:T(8,128)(2,1)S(1)}, u32[]{:S(2)}, u32[]{:S(2)}) collective-permute-start(bf16[4,1,256,256]{3,2,1,0:T(8,128)(2,1)S(1)} %collective-permute-done), channel_id=1, source_target_pairs={{0,1},{1,2},{2,3},{3,4},{4,5},{5,6},{6,7},{7,8},{8,9},{9,10},{10,1... | collective-permute-start | bytes 1572872 | tf_op jit(solution)/shard_map/ppermute | solution.py:19
  25.2 15.5 %collective-permute-start.3 = (bf16[4,1,256,256]{3,2,1,0:T(8,128)(2,1)S(1)}, bf16[4,1,256,256]{3,2,1,0:T(8,128)(2,1)S(1)}, u32[]{:S(2)}, u32[]{:S(2)}) collective-permute-start(bf16[4,1,256,256]{3,2,1,0:T(8,128)(2,1)S(1)} %collective-permute-done.1), channel_id=1, source_target_pairs={{0,15},{1,0},{2,1},{3,2},{4,3},{5,4},{6,5},{7,6},{8,7},{9,8},{10,9... | collective-permute-start | bytes 1572872 | tf_op jit(solution)/shard_map/ppermute | solution.py:24
  40.7 14.6 %copy-start.12 = (bf16[4,1,256,256]{3,2,1,0:T(8,128)(2,1)}, bf16[4,1,256,256]{3,2,1,0:T(8,128)(2,1)S(1)}, u32[]{:S(2)}) copy-start(bf16[4,1,256,256]{3,2,1,0:T(8,128)(2,1)S(1)} %collective-permute-done.2) | copy-start | bytes 1572868
  40.7 14.6 %collective-permute-start.4 = (bf16[4,1,256,256]{3,2,1,0:T(8,128)(2,1)S(1)}, bf16[4,1,256,256]{3,2,1,0:T(8,128)(2,1)S(1)}, u32[]{:S(2)}, u32[]{:S(2)}) collective-permute-start(bf16[4,1,256,256]{3,2,1,0:T(8,128)(2,1)S(1)} %collective-permute-done.2), channel_id=1, source_target_pairs={{0,1},{1,2},{2,3},{3,4},{4,5},{5,6},{6,7},{7,8},{8,9},{9,10},{10,1... | collective-permute-start | bytes 1572872 | tf_op jit(solution)/shard_map/ppermute | solution.py:19
  40.7 50.3 %collective-permute-start.5 = (bf16[4,1,256,256]{3,2,1,0:T(8,128)(2,1)S(1)}, bf16[4,1,256,256]{3,2,1,0:T(8,128)(2,1)S(1)}, u32[]{:S(2)}, u32[]{:S(2)}) collective-permute-start(bf16[4,1,256,256]{3,2,1,0:T(8,128)(2,1)S(1)} %collective-permute-done.3), channel_id=1, source_target_pairs={{0,15},{1,0},{2,1},{3,2},{4,3},{5,4},{6,5},{7,6},{8,7},{9,8},{10,9... | collective-permute-start | bytes 1572872 | tf_op jit(solution)/shard_map/ppermute | solution.py:24
  55.3 36.7 %collective-permute-start.6 = (bf16[4,1,256,256]{3,2,1,0:T(8,128)(2,1)S(1)}, bf16[4,1,256,256]{3,2,1,0:T(8,128)(2,1)}, u32[]{:S(2)}, u32[]{:S(2)}) collective-permute-start(bf16[4,1,256,256]{3,2,1,0:T(8,128)(2,1)S(1)} %collective-permute-done.4), channel_id=1, source_target_pairs={{0,1},{1,2},{2,3},{3,4},{4,5},{5,6},{6,7},{7,8},{8,9},{9,10},{10,1... | collective-permute-start | bytes 1572872 | tf_op jit(solution)/shard_map/ppermute | solution.py:19
  78.4 201.6 %all-to-all-start = ((s32[4,8,2]{0,2,1:T(2,128)}), s32[4,8,2]{0,2,1:T(2,128)S(1)}, u32[]{:S(2)}, u32[]{:S(2)}) async-start(s32[4,8,2]{0,2,1:T(2,128)} %bitcast.3), calls=%async_computation | async-start | bytes 16384 | tf_op jit(solution)/shard_map/all_to_all | solution.py:58
  91.0 13.7 %collective-permute-start.7 = (bf16[4,1,256,256]{3,2,1,0:T(8,128)(2,1)S(1)}, bf16[4,1,256,256]{3,2,1,0:T(8,128)(2,1)}, u32[]{:S(2)}, u32[]{:S(2)}) collective-permute-start(bf16[4,1,256,256]{3,2,1,0:T(8,128)(2,1)S(1)} %collective-permute-done.5), channel_id=1, source_target_pairs={{0,15},{1,0},{2,1},{3,2},{4,3},{5,4},{6,5},{7,6},{8,7},{9,8},{10,9... | collective-permute-start | bytes 1572872 | tf_op jit(solution)/shard_map/ppermute | solution.py:24
  91.9 17.0 %collective-permute-start.8 = (bf16[4,1,256,256]{3,2,1,0:T(8,128)(2,1)}, bf16[4,1,256,256]{3,2,1,0:T(8,128)(2,1)}, u32[]{:S(2)}, u32[]{:S(2)}) collective-permute-start(bf16[4,1,256,256]{3,2,1,0:T(8,128)(2,1)} %collective-permute-done.6), channel_id=1, source_target_pairs={{0,1},{1,2},{2,3},{3,4},{4,5},{5,6},{6,7},{7,8},{8,9},{9,10},{10,1... | collective-permute-start | bytes 1572872 | tf_op jit(solution)/shard_map/ppermute | solution.py:19
  92.6 4.3 copy-start.11
  104.7 15.0 %collective-permute-start.9 = (bf16[4,1,256,256]{3,2,1,0:T(8,128)(2,1)}, bf16[4,1,256,256]{3,2,1,0:T(8,128)(2,1)}, u32[]{:S(2)}, u32[]{:S(2)}) collective-permute-start(bf16[4,1,256,256]{3,2,1,0:T(8,128)(2,1)} %collective-permute-done.7), channel_id=1, source_target_pairs={{0,15},{1,0},{2,1},{3,2},{4,3},{5,4},{6,5},{7,6},{8,7},{9,8},{10,9... | collective-permute-start | bytes 1572872 | tf_op jit(solution)/shard_map/ppermute | solution.py:24
  108.9 17.1 %collective-permute-start.10 = (bf16[4,1,256,256]{3,2,1,0:T(8,128)(2,1)}, bf16[4,1,256,256]{3,2,1,0:T(8,128)(2,1)}, u32[]{:S(2)}, u32[]{:S(2)}) collective-permute-start(bf16[4,1,256,256]{3,2,1,0:T(8,128)(2,1)} %collective-permute-done.8), channel_id=1, source_target_pairs={{0,1},{1,2},{2,3},{3,4},{4,5},{5,6},{6,7},{7,8},{8,9},{9,10},{10,1... | collective-permute-start | bytes 1572872 | tf_op jit(solution)/shard_map/ppermute | solution.py:19
  119.7 15.4 %collective-permute-start.11 = (bf16[4,1,256,256]{3,2,1,0:T(8,128)(2,1)}, bf16[4,1,256,256]{3,2,1,0:T(8,128)(2,1)S(1)}, u32[]{:S(2)}, u32[]{:S(2)}) collective-permute-start(bf16[4,1,256,256]{3,2,1,0:T(8,128)(2,1)} %collective-permute-done.9), channel_id=1, source_target_pairs={{0,15},{1,0},{2,1},{3,2},{4,3},{5,4},{6,5},{7,6},{8,7},{9,8},{10,9... | collective-permute-start | bytes 1572872 | tf_op jit(solution)/shard_map/ppermute | solution.py:24
  126.0 16.3 %collective-permute-start.12 = (bf16[4,1,256,256]{3,2,1,0:T(8,128)(2,1)}, bf16[4,1,256,256]{3,2,1,0:T(8,128)(2,1)S(1)}, u32[]{:S(2)}, u32[]{:S(2)}) collective-permute-start(bf16[4,1,256,256]{3,2,1,0:T(8,128)(2,1)} %collective-permute-done.10), channel_id=1, source_target_pairs={{0,1},{1,2},{2,3},{3,4},{4,5},{5,6},{6,7},{7,8},{8,9},{9,10},{10,1... | collective-permute-start | bytes 1572872 | tf_op jit(solution)/shard_map/ppermute | solution.py:19
  135.1 14.0 %collective-permute-start.13 = (bf16[4,1,256,256]{3,2,1,0:T(8,128)(2,1)S(1)}, bf16[4,1,256,256]{3,2,1,0:T(8,128)(2,1)S(1)}, u32[]{:S(2)}, u32[]{:S(2)}) collective-permute-start(bf16[4,1,256,256]{3,2,1,0:T(8,128)(2,1)S(1)} %collective-permute-done.11), channel_id=1, source_target_pairs={{0,15},{1,0},{2,1},{3,2},{4,3},{5,4},{6,5},{7,6},{8,7},{9,8},{10,9... | collective-permute-start | bytes 1572872 | tf_op jit(solution)/shard_map/ppermute | solution.py:24
  142.4 13.9 %collective-permute-start.14 = (bf16[4,1,256,256]{3,2,1,0:T(8,128)(2,1)S(1)}, bf16[4,1,256,256]{3,2,1,0:T(8,128)(2,1)S(1)}, u32[]{:S(2)}, u32[]{:S(2)}) collective-permute-start(bf16[4,1,256,256]{3,2,1,0:T(8,128)(2,1)S(1)} %collective-permute-done.12), channel_id=1, source_target_pairs={{0,1},{1,2},{2,3},{3,4},{4,5},{5,6},{6,7},{7,8},{8,9},{9,10},{10,1... | collective-permute-start | bytes 1572872 | tf_op jit(solution)/shard_map/ppermute | solution.py:19
  197.9 4.1 copy-start.10
  222.3 4.6 copy-start.13
  226.9 2.0 copy-start.1
  229.0 6.0 copy-start.4
  247.7 4.1 copy-start.3
  262.3 1.6 copy-start.5
  262.3 2.2 copy-start.6
  279.9 8.8 %copy-start.14 = (s32[4]{0:T(128)S(1)}, s32[4]{0:T(128)}, u32[]{:S(2)}) copy-start(s32[4]{0:T(128)} %param.15) | copy-start | bytes 52
  280.0 102.7 %all-to-all-start.1 = ((bf16[4,16,256,256]{3,2,0,1:T(8,128)(2,1)}), bf16[4,16,256,256]{3,2,0,1:T(8,128)(2,1)}, u32[]{:S(2)}, u32[]{:S(2)}) async-start(bf16[4,16,256,256]{3,2,0,1:T(8,128)(2,1)} %copy.45), calls=%async_computation.1 | async-start | bytes 16777216 | tf_op jit(solution)/shard_map/all_to_all | solution.py:57
  288.8 371.5 %all-reduce.3.cloned.1.call-start = ((), (), s32[]{:S(2)}) async-start(), calls=%async_computation.3 | async-start | bytes 16777216
  382.6 7.8 %copy-start.8 = (bf16[32,256,256]{2,1,0:T(8,128)(2,1)S(1)}, bf16[32,256,256]{2,1,0:T(8,128)(2,1)}, u32[]{:S(2)}) copy-start(bf16[32,256,256]{2,1,0:T(8,128)(2,1)} %gather_fusion) | copy-start | bytes 12582916
  390.4 5.8 copy-start.2
  390.4 7.3 %copy-start.7 = (bf16[32,256,256]{2,1,0:T(8,128)(2,1)S(1)}, bf16[32,256,256]{2,1,0:T(8,128)(2,1)}, u32[]{:S(2)}) copy-start(bf16[32,256,256]{2,1,0:T(8,128)(2,1)} %gather_fusion.1) | copy-start | bytes 12582916
  397.8 3.2 copy-start.9
  524.0 0.7 copy-start.16
  524.0 136.3 %copy-start.15 = (s32[4]{0:T(128)S(1)}, s32[4]{0:T(128)}, u32[]{:S(2)}) copy-start(s32[4]{0:T(128)} %param.14) | copy-start | bytes 52
Sparse Core Ops, SparseCore 0:
  524.1 136.0 all-reduce.2
